TPU v7x, 512 devices: a whole 4x8x8 slice. The times are simulated.
512 devices in a mesh: tm: 32 (over z, y_lo, core), depth: 16 (over x, y_hi).
Axes of the slice: x: 4, y: 8 (y_hi: 4, y_lo: 2; y = y_hi * 2 + y_lo), z: 8, core: 2. Of those that a mesh axis runs over, the one named last changes fastest.
Arguments:
- raw: bfloat16 [512, 128, 128], P('tm', 'depth'), may hold values from -6 to 6
- stream: bfloat16 [512, 128, 2048], P('tm', 'depth'), may hold values from -6 to 6
- conv_w: bfloat16 [3, 128, 2048], replicated, may hold values from -0.3125 to 0.3125
- gain: float32 [2048], replicated, may hold values from 0.1 to 1.9
- w_qkv: bfloat16 [2048, 3072], P('tm', 'depth'), may hold values from -4 to 4
- mask: int32 [16, 32, 5], P('depth', 'tm'), may hold values from 0 to 1, as said below
Outputs:
- context: bfloat16 [512, 128, 1024], P('tm', 'depth')
Inputs may be any that keep to these rules, and one draw needn't show every extreme that they name: mask[p, i, 2] = 1 for every block; mask[p, i, e] = 0 wherever i + e - 2 lies outside 0 to 31.
All inputs are finite; a program needn't handle non-finite values.
Results may differ from a plain program's by a relative error of at most 0.012.
The roundings to bfloat16 on the way count: a program that leaves them out, or rounds other values in their place, can miss the bound.
Values may be sent and summed in bfloat16 or wider, within the bound.
A program may use at most 64 MiB of HBM per device.

v0:
```python
import math
import jax
import jax.numpy as jnp
from jax import lax
from jax.sharding import PartitionSpec as P

HEADS = 8
HD = 128
BT = 16
PP = 8
RD = 2


def padded_2(value, sides, width):
    for axis, dim in sides:
        devices, length = (lax.axis_size(axis), value.shape[dim])
        up = [(i, (i + 1) % devices) for i in range(devices - 1)]
        down = [(j, i) for i, j in up]
        last = lax.slice_in_dim(value, length - width, length, axis=dim)
        leading = lax.slice_in_dim(value, 0, width, axis=dim)
        before = lax.ppermute(last, axis, up)
        after = lax.ppermute(leading, axis, down)
        value = jnp.concatenate([before, value, after], axis=dim)
    return value


def from_behind(value, axis, by):
    devices = lax.axis_size(axis)
    pairs = [(i, i + by) for i in range(devices) if 0 <= i + by < devices]
    return lax.ppermute(value, axis, pairs)


def head_attend(query_head, key_head, value_head, allowed):
    inv_root = 1.0 / math.sqrt(HD)
    scores = (
        jnp.einsum("qd,kd->qk", query_head, key_head, preferred_element_type=jnp.float32) * inv_root
    )
    scores = jnp.where(allowed, scores, -1e30)
    row_max = jnp.max(scores, axis=-1, keepdims=True)
    powers = jnp.exp(scores - row_max)
    weights = (powers / jnp.sum(powers, axis=-1, keepdims=True)).astype(jnp.bfloat16)
    return jnp.dot(weights, value_head, preferred_element_type=jnp.float32).astype(jnp.bfloat16)


def per_device(raw, stream, conv_w, gain, w_qkv, mask):
    time_len, site_len, feat_len = raw.shape
    tok_rows = time_len * site_len
    padded = padded_2(raw, (("depth", 1),), 1)
    embedded = stream.reshape(tok_rows, stream.shape[2]).astype(jnp.float32)
    for offset in range(3):
        window = padded[:, offset : offset + site_len].reshape(tok_rows, feat_len)
        embedded = embedded + jnp.dot(window, conv_w[offset], preferred_element_type=jnp.float32)
    normed = (
        embedded * lax.rsqrt(jnp.mean(embedded * embedded, axis=-1, keepdims=True) + 1e-05) * gain
    ).astype(jnp.bfloat16)
    columns = lax.all_gather(w_qkv, "depth", axis=1, tiled=True)
    projected = jnp.dot(
        normed,
        lax.all_gather(columns, "tm", axis=0, tiled=True),
        preferred_element_type=jnp.float32,
    ).astype(jnp.bfloat16)
    head_cols = projected.shape[1] // 3
    queries = projected[:, :head_cols]
    keyvals = projected[:, head_cols:]
    earlier = []
    later = []
    moving_back = keyvals
    moving_ahead = keyvals
    for hop_index in range(RD):
        moving_back = from_behind(moving_back, "tm", 1)
        moving_ahead = from_behind(moving_ahead, "tm", -1)
        earlier.insert(0, moving_back)
        later.append(moving_ahead)
    gathered = jnp.concatenate(earlier + [keyvals] + later, axis=0)
    block_rows = BT * PP
    own_blocks = tok_rows // block_rows
    span_blocks = gathered.shape[0] // block_rows
    local_mask = mask[0]
    query_ids = jnp.arange(own_blocks, dtype=jnp.int32)[:, None]
    key_ids = jnp.arange(span_blocks, dtype=jnp.int32)[None, :]
    entry_ids = key_ids - query_ids
    picks = entry_ids[:, :, None] == jnp.arange(local_mask.shape[1], dtype=jnp.int32)[None, None, :]
    block_allowed = jnp.sum(jnp.where(picks, local_mask[:, None, :], 0), axis=-1) > 0
    allowed = jnp.repeat(jnp.repeat(block_allowed, block_rows, axis=0), block_rows, axis=1)
    query_heads = queries.reshape(tok_rows, HEADS, HD).transpose(1, 0, 2)
    key_heads = gathered[:, :head_cols].reshape(gathered.shape[0], HEADS, HD).transpose(1, 0, 2)
    value_heads = gathered[:, head_cols:].reshape(gathered.shape[0], HEADS, HD).transpose(1, 0, 2)
    context = lax.map(
        lambda operands: head_attend(operands[0], operands[1], operands[2], allowed),
        (query_heads, key_heads, value_heads),
    )
    return context.transpose(1, 0, 2).reshape(time_len, site_len, head_cols)


def solution(mesh):
    in_specs = (
        P("tm", "depth", None),
        P("tm", "depth", None),
        P(),
        P(),
        P("tm", "depth"),
        P("depth", "tm", None),
    )
    out_specs = P("tm", "depth", None)
    return jax.shard_map(
        per_device, mesh=mesh, in_specs=in_specs, out_specs=out_specs, check_vma=False
    )
```

profile of v0, /device:TPU:1, one launch (start us, length us, event | category | flops | bytes accessed | tf_op | source)
XLA Modules:
  0.0 192.2 jit_solution(5119026603187726884)
XLA Ops:
  6.5 0.0 copy-start.2
  6.5 0.0 copy-start
  6.5 0.0 all-gather.3.cloned.1.call-start
  6.5 42.6 %all-gather = bf16[16,192,64]{1,2,0:T(8,128)(2,1)S(1)} all-gather(bf16[1,192,64]{1,2,0:T(8,128)(2,1)} %bitcast.82), channel_id=1, replica_groups=mesh['tm'=32,'depth'=16] {'depth'}, dimensions={0}, use_global_device_ids=true | all-gather | bytes 417792 | tf_op jit(solution)/shard_map/all_gather | solution.py:56
  49.1 0.3 copy.21
  49.4 0.0 copy-start.1
  49.4 1.3 reshape.102
  50.8 0.0 all-gather.3.cloned.1.call-update
  50.8 0.0 copy-done.2
  50.8 1.3 collective-permute-start
  52.1 1.3 collective-permute-start.1
  53.4 0.0 copy-done
  53.4 0.3 fusion.18
  53.7 0.0 collective-permute-done
  53.7 0.0 copy-done.1
  53.7 0.3 fusion.16
  54.0 0.0 copy-start.4
  54.0 3.4 %collective-permute-done.1 = bf16[16,1,128]{2,1,0:T(2,128)(2,1)S(1)} collective-permute-done((bf16[16,1,128]{2,1,0:T(2,128)(2,1)S(1)}, bf16[16,1,128]{2,1,0:T(2,128)(2,1)S(1)}, u32[]{:S(2)}, u32[]{:S(2)}) %collective-permute-start.1) | collective-permute-done | bytes 4128 | tf_op jit(solution)/shard_map/ppermute | solution.py:22
  57.4 0.4 multiply_reduce_fusion
  57.8 80.7 %all-gather.3.cloned.1.call-done = bf16[2048,3072]{1,0:T(8,128)(2,1)} async-done(((bf16[64,3072]{1,0:T(8,128)(2,1)}), bf16[2048,3072]{1,0:T(8,128)(2,1)}) %all-gather.3.cloned.1.call-update) | async-done | bytes 12582928 | tf_op jit(solution)/shard_map/all_gather | solution.py:59
  138.5 0.0 copy-done.4
  138.5 6.5 %convolution_convert_fusion.1 = bf16[128,3072]{1,0:T(8,128)(2,1)S(1)} fusion(bf16[2048,3072]{1,0:T(8,128)(2,1)} %all-gather.3.cloned.1.call-done, f32[128,2048]{1,0:T(8,128)S(1)} %get-tuple-element.72, f32[2048]{0:T(1024)S(1)} %copy-done.4, f32[128]{0:T(128)S(1)} %add_rsqrt_fusion), kind=kOutput, calls=%fused_computation.19 | convolution fusion | flops 1611792384 | bytes 14426624 | tf_op jit(solution)/shard_map/dot_general | solution.py:57
  145.0 2.9 %collective-permute-start.2 = (bf16[128,2048]{1,0:T(8,128)(2,1)S(1)}, bf16[128,2048]{1,0:T(8,128)(2,1)S(1)}, u32[]{:S(2)}, u32[]{:S(2)}) collective-permute-start(bf16[128,2048]{1,0:T(8,128)(2,1)S(1)} %slice.47), channel_id=1, source_target_pairs={{0,16},{16,32},{32,48},{48,64},{64,80},{80,96},{96,112},{112,128},... | collective-permute-start | bytes 1572872 | tf_op jit(solution)/shard_map/ppermute | solution.py:30
  147.9 0.0 copy-done.5
  148.0 0.2 fusion.33
  148.1 1.9 collective-permute-start.4
  150.1 4.0 %collective-permute-done.2 = bf16[128,2048]{1,0:T(8,128)(2,1)S(1)} collective-permute-done((bf16[128,2048]{1,0:T(8,128)(2,1)S(1)}, bf16[128,2048]{1,0:T(8,128)(2,1)S(1)}, u32[]{:S(2)}, u32[]{:S(2)}) %collective-permute-start.2) | collective-permute-done | bytes 524320 | tf_op jit(solution)/shard_map/ppermute | solution.py:30
  154.1 4.4 %collective-permute-start.3 = (bf16[128,2048]{1,0:T(8,128)(2,1)S(1)}, bf16[128,2048]{1,0:T(8,128)(2,1)S(1)}, u32[]{:S(2)}, u32[]{:S(2)}) collective-permute-start(bf16[128,2048]{1,0:T(8,128)(2,1)S(1)} %collective-permute-done.2), channel_id=1, source_target_pairs={{0,16},{16,32},{32,48},{48,64},{64,80},{80,96},{96,112},{112,128},... | collective-permute-start | bytes 1572872 | tf_op jit(solution)/shard_map/ppermute | solution.py:30
  158.5 0.1 broadcast_bitcast_fusion
  158.6 3.1 %collective-permute-done.4 = bf16[128,2048]{1,0:T(8,128)(2,1)S(1)} collective-permute-done((bf16[128,2048]{1,0:T(8,128)(2,1)S(1)}, bf16[128,2048]{1,0:T(8,128)(2,1)S(1)}, u32[]{:S(2)}, u32[]{:S(2)}) %collective-permute-start.4) | collective-permute-done | bytes 524320 | tf_op jit(solution)/shard_map/ppermute | solution.py:30
  161.7 1.9 collective-permute-start.5
  163.6 0.9 collective-permute-done.3
  164.7 11.3 %collective-permute-done.5 = bf16[128,2048]{1,0:T(8,128)(2,1)S(1)} collective-permute-done((bf16[128,2048]{1,0:T(8,128)(2,1)S(1)}, bf16[128,2048]{1,0:T(8,128)(2,1)S(1)}, u32[]{:S(2)}, u32[]{:S(2)}) %collective-permute-start.5) | collective-permute-done | bytes 524320 | tf_op jit(solution)/shard_map/ppermute | solution.py:30
  176.1 0.7 slice_bitcast_fusion
  176.8 0.0 copy-start.3
  176.8 0.6 bitcast_bitcast_fusion
  177.4 0.3 copy-done.3
  177.7 6.6 %while.11 = (s32[]{:T(128)}, bf16[8,128,128]{2,1,0:T(8,128)(2,1)S(1)}, bf16[8,128,128]{2,1,0:T(8,128)(2,1)S(1)}, bf16[8,640,128]{2,1,0:T(8,128)(2,1)S(1)}, bf16[...) while((s32[]{:T(128)}, bf16[8,128,128]{2,1,0:T(8,128)(2,1)S(1)}, ...), condition=%wide.region_5.6_spmd.clone, body=%wide.region_2.5_spmd.clone.sunk | while | flops 42614528 | bytes 1381965 | solution.py:88
  177.7 0.3 fusion.44
  178.0 0.2 fusion.45
  178.2 0.3 fusion.46
  178.6 0.3 fusion.44
  178.9 0.2 fusion.45
  179.1 0.3 fusion.46
  179.4 0.3 fusion.44
  179.7 0.2 fusion.45
  179.9 0.3 fusion.46
  180.2 0.3 fusion.44
  180.5 0.2 fusion.45
  180.7 0.3 fusion.46
  181.0 0.3 fusion.44
  181.3 0.2 fusion.45
  181.6 0.3 fusion.46
  181.9 0.3 fusion.44
  182.2 0.2 fusion.45
  182.4 0.3 fusion.46
  182.7 0.3 fusion.44
  183.0 0.2 fusion.45
  183.2 0.3 fusion.46
  183.5 0.3 fusion.44
  183.8 0.2 fusion.45
  184.0 0.3 fusion.46
  184.3 0.2 copy.25
  184.5 0.8 reshape.99
  (12 shorter events, 0.3 us)
Async XLA Ops:
  6.5 44.2 %copy-start.2 = (bf16[16,8,128]{2,1,0:T(8,128)(2,1)S(1)}, bf16[16,8,128]{2,1,0:T(8,128)(2,1)}, u32[]{:S(2)}) copy-start(bf16[16,8,128]{2,1,0:T(8,128)(2,1)} %param.8) | copy-start | bytes 98308
  6.5 46.9 %copy-start = (bf16[3,128,2048]{2,1,0:T(8,128)(2,1)S(1)}, bf16[3,128,2048]{2,1,0:T(8,128)(2,1)}, u32[]{:S(2)}) copy-start(bf16[3,128,2048]{2,1,0:T(8,128)(2,1)} %param.10) | copy-start | bytes 4718596
  6.5 132.0 %all-gather.3.cloned.1.call-start = ((), (), s32[]{:S(2)}) async-start(), calls=%async_computation | async-start | bytes 12976128 | tf_op jit(solution)/shard_map/all_gather | solution.py:59
  49.4 4.3 %copy-start.1 = (bf16[16,8,2048]{2,1,0:T(8,128)(2,1)S(1)}, bf16[16,8,2048]{2,1,0:T(8,128)(2,1)}, u32[]{:S(2)}) copy-start(bf16[16,8,2048]{2,1,0:T(8,128)(2,1)} %param.9) | copy-start | bytes 1572868
  50.8 2.9 %collective-permute-start = (bf16[16,1,128]{2,1,0:T(2,128)(2,1)S(1)}, bf16[16,1,128]{2,1,0:T(2,128)(2,1)S(1)}, u32[]{:S(2)}, u32[]{:S(2)}) collective-permute-start(bf16[16,1,128]{2,1,0:T(2,128)(2,1)S(1)} %get-tuple-element.70), channel_id=1, source_target_pairs={{0,1},{1,2},{2,3},{3,4},{4,5},{5,6},{6,7},{7,8},{8,9},{9,10},{10,1... | collective-permute-start | bytes 12296 | tf_op jit(solution)/shard_map/ppermute | solution.py:21
  52.1 5.3 %collective-permute-start.1 = (bf16[16,1,128]{2,1,0:T(2,128)(2,1)S(1)}, bf16[16,1,128]{2,1,0:T(2,128)(2,1)S(1)}, u32[]{:S(2)}, u32[]{:S(2)}) collective-permute-start(bf16[16,1,128]{2,1,0:T(2,128)(2,1)S(1)} %get-tuple-element.69), channel_id=1, source_target_pairs={{1,0},{2,1},{3,2},{4,3},{5,4},{6,5},{7,6},{8,7},{9,8},{10,9},{11,1... | collective-permute-start | bytes 12296 | tf_op jit(solution)/shard_map/ppermute | solution.py:22
  54.0 84.5 %copy-start.4 = (f32[2048]{0:T(1024)S(1)}, f32[2048]{0:T(1024)}, u32[]{:S(2)}) copy-start(f32[2048]{0:T(1024)} %param.11) | copy-start | bytes 24580
  138.5 9.4 %copy-start.5 = (s32[1,1,5]{2,1,0:T(1,128)S(1)}, s32[1,1,5]{2,1,0:T(1,128)}, u32[]{:S(2)}) copy-start(s32[1,1,5]{2,1,0:T(1,128)} %param.13) | copy-start | bytes 64
  145.0 9.0 %collective-permute-start.2 = (bf16[128,2048]{1,0:T(8,128)(2,1)S(1)}, bf16[128,2048]{1,0:T(8,128)(2,1)S(1)}, u32[]{:S(2)}, u32[]{:S(2)}) collective-permute-start(bf16[128,2048]{1,0:T(8,128)(2,1)S(1)} %slice.47), channel_id=1, source_target_pairs={{0,16},{16,32},{32,48},{48,64},{64,80},{80,96},{96,112},{112,128},... | collective-permute-start | bytes 1572872 | tf_op jit(solution)/shard_map/ppermute | solution.py:30
  148.1 13.5 %collective-permute-start.4 = (bf16[128,2048]{1,0:T(8,128)(2,1)S(1)}, bf16[128,2048]{1,0:T(8,128)(2,1)S(1)}, u32[]{:S(2)}, u32[]{:S(2)}) collective-permute-start(bf16[128,2048]{1,0:T(8,128)(2,1)S(1)} %slice.47), channel_id=1, source_target_pairs={{16,0},{32,16},{48,32},{64,48},{80,64},{96,80},{112,96},{128,112},... | collective-permute-start | bytes 1572872 | tf_op jit(solution)/shard_map/ppermute | solution.py:30
  154.1 10.5 %collective-permute-start.3 = (bf16[128,2048]{1,0:T(8,128)(2,1)S(1)}, bf16[128,2048]{1,0:T(8,128)(2,1)S(1)}, u32[]{:S(2)}, u32[]{:S(2)}) collective-permute-start(bf16[128,2048]{1,0:T(8,128)(2,1)S(1)} %collective-permute-done.2), channel_id=1, source_target_pairs={{0,16},{16,32},{32,48},{48,64},{64,80},{80,96},{96,112},{112,128},... | collective-permute-start | bytes 1572872 | tf_op jit(solution)/shard_map/ppermute | solution.py:30
  161.7 14.4 %collective-permute-start.5 = (bf16[128,2048]{1,0:T(8,128)(2,1)S(1)}, bf16[128,2048]{1,0:T(8,128)(2,1)S(1)}, u32[]{:S(2)}, u32[]{:S(2)}) collective-permute-start(bf16[128,2048]{1,0:T(8,128)(2,1)S(1)} %collective-permute-done.4), channel_id=1, source_target_pairs={{16,0},{32,16},{48,32},{64,48},{80,64},{96,80},{112,96},{128,112},... | collective-permute-start | bytes 1572872 | tf_op jit(solution)/shard_map/ppermute | solution.py:30
  176.8 1.0 copy-start.3
Sparse Core Ops, SparseCore 0:
  50.9 87.5 all-gather.2
where the time goes:
time: 192 us
  waiting for transfers between devices  103 us (54%)
  blocking collectives  42.6 us (22%)
  starting transfers between devices  13.7 us (7%)
  between operations  13.6 us (7%)
  matrix products  12.1 us (6%)
  local copies, waits for them, and re-layouts  4.61 us (2%)
    all_gather x1, waiting for transfers between devices, per_device(): lax.all_gather(columns, 'tm', axis=0, tiled=True)  80.7 us
    all_gather x1, blocking collectives, per_device(): columns = lax.all_gather(w_qkv, 'depth', axis=1, tiled=True)  42.6 us
    ppermute x4, waiting for transfers between devices, from_behind(): return lax.ppermute(value, axis, pairs)  19.3 us
    ppermute x4, starting transfers between devices, from_behind(): return lax.ppermute(value, axis, pairs)  11.1 us
    dot_general x1, matrix products, per_device(): jnp.dot(normed, lax.all_gather(columns, 'tm', axis=0, tiled=True), prefer...  6.45 us
  transfers between devices with their start and end apart: 7, of which 6 were waited for; matrix products, arithmetic and copies ran while one was open for 1% of the time, Pallas kernels for 0%

commit v1 on v0

--- a/solution.py
+++ b/solution.py
@@ -53,7 +53,10 @@
     normed = (
         embedded * lax.rsqrt(jnp.mean(embedded * embedded, axis=-1, keepdims=True) + 1e-05) * gain
     ).astype(jnp.bfloat16)
-    columns = lax.all_gather(w_qkv, "depth", axis=1, tiled=True)
+    size = lax.axis_size("depth")
+    blocks = jnp.stack([w_qkv for _ in range(size)])
+    blocks = lax.all_to_all(blocks, "depth", split_axis=0, concat_axis=0)
+    columns = jnp.concatenate(blocks, axis=1)
     projected = jnp.dot(
         normed,
         lax.all_gather(columns, "tm", axis=0, tiled=True),

time: 192 us -> 174 us (0.906)
  blocking collectives: 42.6 us -> 27.4 us
  waiting for transfers between devices: 103 us -> 97 us
  starting transfers between devices: 13.7 us -> 16.1 us
    all_gather x1 -> x0, blocking collectives: 42.6 us -> none  [per_device(): columns = lax.all_gather(w_qkv, 'depth', axis=1, tiled=True)]
    all_to_all x0 -> x1, blocking collectives: none -> 27.4 us  [per_device(): blocks = lax.all_to_all(blocks, 'depth', split_axis=0, concat_axis=0)]
    all_gather x1, waiting for transfers between devices: 80.7 us -> 74.4 us  [per_device(): lax.all_gather(columns, 'tm', axis=0, tiled=True)]
    ppermute x1, starting transfers between devices: 1.29 us -> 3.6 us  [padded_2(): before = lax.ppermute(last, axis, up)]
where the time goes in v1:
time: 174 us
  waiting for transfers between devices  97 us (56%)
  blocking collectives  27.4 us (16%)
  starting transfers between devices  16.1 us (9%)
  between operations  13.7 us (8%)
  matrix products  12.1 us (7%)
  local copies, waits for them, and re-layouts  5.41 us (3%)
  other arithmetic  1.87 us (1%)
    all_gather x1, waiting for transfers between devices, per_device(): lax.all_gather(columns, 'tm', axis=0, tiled=True)  74.4 us
    all_to_all x1, blocking collectives, per_device(): blocks = lax.all_to_all(blocks, 'depth', split_axis=0, concat_axis=0)  27.4 us
    ppermute x4, waiting for transfers between devices, from_behind(): return lax.ppermute(value, axis, pairs)  19.3 us
    ppermute x4, starting transfers between devices, from_behind(): return lax.ppermute(value, axis, pairs)  11.2 us
    dot_general x1, matrix products, per_device(): jnp.dot(normed, lax.all_gather(columns, 'tm', axis=0, tiled=True), prefer...  6.45 us
    ppermute x1, starting transfers between devices, padded_2(): before = lax.ppermute(last, axis, up)  3.6 us
  transfers between devices with their start and end apart: 7, of which 6 were waited for; matrix products, arithmetic and copies ran while one was open for 1% of the time, Pallas kernels for 0%

profile of v1, /device:TPU:1, one launch (start us, length us, event | category | flops | bytes accessed | tf_op | source)
XLA Modules:
  0.0 173.8 jit_solution(15164344969350926737)
XLA Ops:
  6.5 0.0 all-gather.2.cloned.1.call-start
  6.5 0.8 stack.2
  7.3 0.0 copy-start.2
  7.4 0.0 copy-start
  7.4 27.4 %all_to_all.5 = bf16[16,64,192]{2,1,0:T(8,128)(2,1)S(1)} all-to-all(bf16[16,64,192]{2,1,0:T(8,128)(2,1)S(1)} %stack.2), channel_id=1, replica_groups=mesh['tm'=32,'depth'=16] {'depth'}, dimensions={0} | all-to-all | bytes 786432 | tf_op jit(solution)/shard_map/all_to_all | solution.py:58
  34.7 0.3 copy.20
  35.0 0.0 copy-start.1
  35.1 1.3 reshape.105
  36.4 0.0 all-gather.2.cloned.1.call-update
  36.4 0.0 copy-done.2
  36.4 3.6 %collective-permute-start = (bf16[16,1,128]{2,1,0:T(2,128)(2,1)S(1)}, bf16[16,1,128]{2,1,0:T(2,128)(2,1)S(1)}, u32[]{:S(2)}, u32[]{:S(2)}) collective-permute-start(bf16[16,1,128]{2,1,0:T(2,128)(2,1)S(1)} %get-tuple-element.70), channel_id=1, source_target_pairs={{0,1},{1,2},{2,3},{3,4},{4,5},{5,6},{6,7},{7,8},{8,9},{9,10},{10,1... | collective-permute-start | bytes 12296 | tf_op jit(solution)/shard_map/ppermute | solution.py:21
  40.0 1.3 collective-permute-start.1
  41.3 0.0 copy-done
  41.3 0.3 fusion.18
  41.6 0.0 collective-permute-done
  41.6 0.0 copy-done.1
  41.7 0.3 fusion.16
  42.0 0.0 copy-start.4
  42.0 3.4 %collective-permute-done.1 = bf16[16,1,128]{2,1,0:T(2,128)(2,1)S(1)} collective-permute-done((bf16[16,1,128]{2,1,0:T(2,128)(2,1)S(1)}, bf16[16,1,128]{2,1,0:T(2,128)(2,1)S(1)}, u32[]{:S(2)}, u32[]{:S(2)}) %collective-permute-start.1) | collective-permute-done | bytes 4128 | tf_op jit(solution)/shard_map/ppermute | solution.py:22
  45.3 0.4 multiply_reduce_fusion
  45.7 74.4 %all-gather.2.cloned.1.call-done = bf16[2048,3072]{1,0:T(8,128)(2,1)} async-done(((bf16[64,3072]{1,0:T(8,128)(2,1)}), bf16[2048,3072]{1,0:T(8,128)(2,1)}) %all-gather.2.cloned.1.call-update) | async-done | bytes 12582928 | tf_op jit(solution)/shard_map/all_gather | solution.py:62
  120.1 0.0 copy-done.4
  120.1 6.5 %convolution_convert_fusion.1 = bf16[128,3072]{1,0:T(8,128)(2,1)S(1)} fusion(bf16[2048,3072]{1,0:T(8,128)(2,1)} %all-gather.2.cloned.1.call-done, f32[128,2048]{1,0:T(8,128)S(1)} %get-tuple-element.72, f32[2048]{0:T(1024)S(1)} %copy-done.4, f32[128]{0:T(128)S(1)} %add_rsqrt_fusion), kind=kOutput, calls=%fused_computation.19 | convolution fusion | flops 1611792384 | bytes 14426624 | tf_op jit(solution)/shard_map/dot_general | solution.py:60
  126.6 3.0 %collective-permute-start.2 = (bf16[128,2048]{1,0:T(8,128)(2,1)S(1)}, bf16[128,2048]{1,0:T(8,128)(2,1)S(1)}, u32[]{:S(2)}, u32[]{:S(2)}) collective-permute-start(bf16[128,2048]{1,0:T(8,128)(2,1)S(1)} %slice.47), channel_id=1, source_target_pairs={{0,16},{16,32},{32,48},{48,64},{64,80},{80,96},{96,112},{112,128},... | collective-permute-start | bytes 1572872 | tf_op jit(solution)/shard_map/ppermute | solution.py:30
  129.6 0.2 fusion.33
  129.8 1.9 %collective-permute-start.4 = (bf16[128,2048]{1,0:T(8,128)(2,1)S(1)}, bf16[128,2048]{1,0:T(8,128)(2,1)S(1)}, u32[]{:S(2)}, u32[]{:S(2)}) collective-permute-start(bf16[128,2048]{1,0:T(8,128)(2,1)S(1)} %slice.47), channel_id=1, source_target_pairs={{16,0},{32,16},{48,32},{64,48},{80,64},{96,80},{112,96},{128,112},... | collective-permute-start | bytes 1572872 | tf_op jit(solution)/shard_map/ppermute | solution.py:30
  131.7 4.0 %collective-permute-done.2 = bf16[128,2048]{1,0:T(8,128)(2,1)S(1)} collective-permute-done((bf16[128,2048]{1,0:T(8,128)(2,1)S(1)}, bf16[128,2048]{1,0:T(8,128)(2,1)S(1)}, u32[]{:S(2)}, u32[]{:S(2)}) %collective-permute-start.2) | collective-permute-done | bytes 524320 | tf_op jit(solution)/shard_map/ppermute | solution.py:30
  135.7 4.4 %collective-permute-start.3 = (bf16[128,2048]{1,0:T(8,128)(2,1)S(1)}, bf16[128,2048]{1,0:T(8,128)(2,1)S(1)}, u32[]{:S(2)}, u32[]{:S(2)}) collective-permute-start(bf16[128,2048]{1,0:T(8,128)(2,1)S(1)} %collective-permute-done.2), channel_id=1, source_target_pairs={{0,16},{16,32},{32,48},{48,64},{64,80},{80,96},{96,112},{112,128},... | collective-permute-start | bytes 1572872 | tf_op jit(solution)/shard_map/ppermute | solution.py:30
  140.1 0.1 broadcast_bitcast_fusion
  140.3 3.1 %collective-permute-done.4 = bf16[128,2048]{1,0:T(8,128)(2,1)S(1)} collective-permute-done((bf16[128,2048]{1,0:T(8,128)(2,1)S(1)}, bf16[128,2048]{1,0:T(8,128)(2,1)S(1)}, u32[]{:S(2)}, u32[]{:S(2)}) %collective-permute-start.4) | collective-permute-done | bytes 524320 | tf_op jit(solution)/shard_map/ppermute | solution.py:30
  143.3 1.9 %collective-permute-start.5 = (bf16[128,2048]{1,0:T(8,128)(2,1)S(1)}, bf16[128,2048]{1,0:T(8,128)(2,1)S(1)}, u32[]{:S(2)}, u32[]{:S(2)}) collective-permute-start(bf16[128,2048]{1,0:T(8,128)(2,1)S(1)} %collective-permute-done.4), channel_id=1, source_target_pairs={{16,0},{32,16},{48,32},{64,48},{80,64},{96,80},{112,96},{128,112},... | collective-permute-start | bytes 1572872 | tf_op jit(solution)/shard_map/ppermute | solution.py:30
  145.2 1.0 collective-permute-done.3
  146.4 11.2 %collective-permute-done.5 = bf16[128,2048]{1,0:T(8,128)(2,1)S(1)} collective-permute-done((bf16[128,2048]{1,0:T(8,128)(2,1)S(1)}, bf16[128,2048]{1,0:T(8,128)(2,1)S(1)}, u32[]{:S(2)}, u32[]{:S(2)}) %collective-permute-start.5) | collective-permute-done | bytes 524320 | tf_op jit(solution)/shard_map/ppermute | solution.py:30
  157.7 0.7 slice_bitcast_fusion
  158.4 0.0 copy-start.3
  158.4 0.6 bitcast_bitcast_fusion
  159.0 0.3 copy-done.3
  159.3 6.6 %while.11 = (s32[]{:T(128)}, bf16[8,128,128]{2,1,0:T(8,128)(2,1)S(1)}, bf16[8,128,128]{2,1,0:T(8,128)(2,1)S(1)}, bf16[8,640,128]{2,1,0:T(8,128)(2,1)S(1)}, bf16[...) while((s32[]{:T(128)}, bf16[8,128,128]{2,1,0:T(8,128)(2,1)S(1)}, ...), condition=%wide.region_5.6_spmd.clone, body=%wide.region_2.5_spmd.clone.sunk | while | flops 42614528 | bytes 1381965 | solution.py:91
  159.3 0.3 fusion.44
  159.6 0.2 fusion.45
  159.8 0.3 fusion.46
  160.2 0.3 fusion.44
  160.5 0.2 fusion.45
  160.7 0.3 fusion.46
  161.0 0.3 fusion.44
  161.3 0.2 fusion.45
  161.5 0.3 fusion.46
  161.8 0.3 fusion.44
  162.1 0.2 fusion.45
  162.3 0.3 fusion.46
  162.6 0.3 fusion.44
  162.9 0.2 fusion.45
  163.1 0.3 fusion.46
  163.5 0.3 fusion.44
  163.8 0.2 fusion.45
  164.0 0.3 fusion.46
  164.3 0.3 fusion.44
  164.6 0.2 fusion.45
  164.8 0.3 fusion.46
  165.1 0.3 fusion.44
  165.4 0.2 fusion.45
  165.6 0.3 fusion.46
  165.9 0.2 copy.24
  166.1 0.8 reshape.109
  (13 shorter events, 0.3 us)
Async XLA Ops:
  6.5 113.5 %all-gather.2.cloned.1.call-start = ((), (), s32[]{:S(2)}) async-start(), calls=%async_computation.1 | async-start | bytes 12976128 | tf_op jit(solution)/shard_map/all_gather | solution.py:62
  7.3 29.1 %copy-start.2 = (bf16[16,8,128]{2,1,0:T(8,128)(2,1)S(1)}, bf16[16,8,128]{2,1,0:T(8,128)(2,1)}, u32[]{:S(2)}) copy-start(bf16[16,8,128]{2,1,0:T(8,128)(2,1)} %param.8) | copy-start | bytes 98308
  7.4 34.0 %copy-start = (bf16[3,128,2048]{2,1,0:T(8,128)(2,1)S(1)}, bf16[3,128,2048]{2,1,0:T(8,128)(2,1)}, u32[]{:S(2)}) copy-start(bf16[3,128,2048]{2,1,0:T(8,128)(2,1)} %param.10) | copy-start | bytes 4718596
  35.0 6.6 %copy-start.1 = (bf16[16,8,2048]{2,1,0:T(8,128)(2,1)S(1)}, bf16[16,8,2048]{2,1,0:T(8,128)(2,1)}, u32[]{:S(2)}) copy-start(bf16[16,8,2048]{2,1,0:T(8,128)(2,1)} %param.9) | copy-start | bytes 1572868
  36.4 5.2 %collective-permute-start = (bf16[16,1,128]{2,1,0:T(2,128)(2,1)S(1)}, bf16[16,1,128]{2,1,0:T(2,128)(2,1)S(1)}, u32[]{:S(2)}, u32[]{:S(2)}) collective-permute-start(bf16[16,1,128]{2,1,0:T(2,128)(2,1)S(1)} %get-tuple-element.70), channel_id=1, source_target_pairs={{0,1},{1,2},{2,3},{3,4},{4,5},{5,6},{6,7},{7,8},{8,9},{9,10},{10,1... | collective-permute-start | bytes 12296 | tf_op jit(solution)/shard_map/ppermute | solution.py:21
  40.0 5.3 %collective-permute-start.1 = (bf16[16,1,128]{2,1,0:T(2,128)(2,1)S(1)}, bf16[16,1,128]{2,1,0:T(2,128)(2,1)S(1)}, u32[]{:S(2)}, u32[]{:S(2)}) collective-permute-start(bf16[16,1,128]{2,1,0:T(2,128)(2,1)S(1)} %get-tuple-element.69), channel_id=1, source_target_pairs={{1,0},{2,1},{3,2},{4,3},{5,4},{6,5},{7,6},{8,7},{9,8},{10,9},{11,1... | collective-permute-start | bytes 12296 | tf_op jit(solution)/shard_map/ppermute | solution.py:22
  42.0 78.1 %copy-start.4 = (f32[2048]{0:T(1024)S(1)}, f32[2048]{0:T(1024)}, u32[]{:S(2)}) copy-start(f32[2048]{0:T(1024)} %param.11) | copy-start | bytes 24580
  120.1 9.6 %copy-start.5 = (s32[1,1,5]{2,1,0:T(1,128)S(1)}, s32[1,1,5]{2,1,0:T(1,128)}, u32[]{:S(2)}) copy-start(s32[1,1,5]{2,1,0:T(1,128)} %param.13) | copy-start | bytes 64
  126.6 9.2 %collective-permute-start.2 = (bf16[128,2048]{1,0:T(8,128)(2,1)S(1)}, bf16[128,2048]{1,0:T(8,128)(2,1)S(1)}, u32[]{:S(2)}, u32[]{:S(2)}) collective-permute-start(bf16[128,2048]{1,0:T(8,128)(2,1)S(1)} %slice.47), channel_id=1, source_target_pairs={{0,16},{16,32},{32,48},{48,64},{64,80},{80,96},{96,112},{112,128},... | collective-permute-start | bytes 1572872 | tf_op jit(solution)/shard_map/ppermute | solution.py:30
  129.8 13.5 %collective-permute-start.4 = (bf16[128,2048]{1,0:T(8,128)(2,1)S(1)}, bf16[128,2048]{1,0:T(8,128)(2,1)S(1)}, u32[]{:S(2)}, u32[]{:S(2)}) collective-permute-start(bf16[128,2048]{1,0:T(8,128)(2,1)S(1)} %slice.47), channel_id=1, source_target_pairs={{16,0},{32,16},{48,32},{64,48},{80,64},{96,80},{112,96},{128,112},... | collective-permute-start | bytes 1572872 | tf_op jit(solution)/shard_map/ppermute | solution.py:30
  135.7 10.5 %collective-permute-start.3 = (bf16[128,2048]{1,0:T(8,128)(2,1)S(1)}, bf16[128,2048]{1,0:T(8,128)(2,1)S(1)}, u32[]{:S(2)}, u32[]{:S(2)}) collective-permute-start(bf16[128,2048]{1,0:T(8,128)(2,1)S(1)} %collective-permute-done.2), channel_id=1, source_target_pairs={{0,16},{16,32},{32,48},{48,64},{64,80},{80,96},{96,112},{112,128},... | collective-permute-start | bytes 1572872 | tf_op jit(solution)/shard_map/ppermute | solution.py:30
  143.3 14.3 %collective-permute-start.5 = (bf16[128,2048]{1,0:T(8,128)(2,1)S(1)}, bf16[128,2048]{1,0:T(8,128)(2,1)S(1)}, u32[]{:S(2)}, u32[]{:S(2)}) collective-permute-start(bf16[128,2048]{1,0:T(8,128)(2,1)S(1)} %collective-permute-done.4), channel_id=1, source_target_pairs={{16,0},{32,16},{48,32},{64,48},{80,64},{96,80},{112,96},{128,112},... | collective-permute-start | bytes 1572872 | tf_op jit(solution)/shard_map/ppermute | solution.py:30
  158.4 1.0 copy-start.3
Sparse Core Ops, SparseCore 0:
  36.5 83.5 all-gather.1
